TPU v7x, 512 devices: a whole 4x8x8 slice. The times are simulated.
512 devices in a mesh: dp: 64 (over x, z, core), tensor: 8 (over y).
Axes of the slice: x: 4, y: 8, z: 8, core: 2. Of those that a mesh axis runs over, the one named last changes fastest.
Arguments:
- q_new: bfloat16 [8192, 8192], P(('dp', 'tensor')), may hold values from -6 to 6
- k_new: bfloat16 [8192, 1024], P(('dp', 'tensor')), may hold values from -8 to 8
- v_new: bfloat16 [8192, 1024], P(('dp', 'tensor')), may hold values from -6 to 6
- hist_kv: bfloat16 [2048, 128, 2, 1024], P('dp', None, None, 'tensor'), may hold values from -8 to 8
- sources: int32 [64, 64, 1], P('dp'), may hold values from 0 to 63; in each aligned block of 64 rows (0 to 63, 64 to 127, ..., all dimensions but the last counted through in order) at most 2 rows name the same one
- block_ids: int32 [64, 64], P('dp'), may hold values from 0 to 31
- hist_len: int32 [64], P('dp'), may hold values from 1 to 64, 3840 in all
Outputs:
- attended: bfloat16 [8192, 8192], P(('dp', 'tensor'))
Inputs may be any that keep to these rules, and one draw needn't show every extreme that they name: `sources`: in each group's list no owner is named in more than 2 slots, and some owner is named in exactly 2 slots. `hist_len`: some group has all 64 slots live.
All inputs are finite; a program needn't handle non-finite values.
Results may differ from a plain program's by a relative error of at most 0.0032.
Values may be sent and summed in bfloat16 or wider, within the bound.
No kernel may reach another device: no remote copies, remote signals or barrier semaphores. Data moves between devices by JAX's collectives and lax.ppermute only.
A program may use at most 64 MiB of HBM per device.

v0:
```python
import math
import jax
import jax.numpy as jnp
from jax import lax
from jax.sharding import PartitionSpec as P

HQ = 64
KVH = 8
HD = 128


def slot_ranks(src_rows):
    count = src_rows.shape[-1]
    order = jnp.arange(count)
    earlier = order[None, :] < order[:, None]
    same = (src_rows[..., :, None] == src_rows[..., None, :]) & earlier
    return jnp.sum(same.astype(jnp.int32), axis=-1)


def owner_table(src_rows, id_rows, ranks, owners, capacity):
    match_owner = src_rows[..., None, :] == owners[:, None]
    slot_index = jnp.arange(capacity)
    match_rank = ranks[..., None, :] == slot_index[:, None]
    hitting = match_owner[..., :, None, :] & match_rank[..., None, :, :]
    return jnp.sum(jnp.where(hitting, id_rows[..., None, None, :], 0), axis=-1)


def local(q_new, k_new, v_new, hist_kv, sources, block_ids, hist_len):
    parts = lax.axis_size("tensor")
    groups = lax.axis_size("dp")
    tok_local, q_width = q_new.shape
    kv_width = k_new.shape[1]
    q_parts = q_new.reshape(tok_local, parts, q_width // parts)
    k_parts = k_new.reshape(tok_local, parts, kv_width // parts)
    v_parts = v_new.reshape(tok_local, parts, kv_width // parts)
    q_here, key_local_part, v_here = (
        lax.all_to_all(q_parts, "tensor", split_axis=1, concat_axis=0, tiled=True),
        lax.all_to_all(k_parts, "tensor", split_axis=1, concat_axis=0, tiled=True),
        lax.all_to_all(v_parts, "tensor", split_axis=1, concat_axis=0, tiled=True),
    )
    new_count = q_here.shape[0]
    kv_heads = kv_width // parts // HD
    per_kv = HQ // KVH
    query_rows = q_here.reshape(new_count, kv_heads, per_kv, HD)
    src_list = sources.reshape(-1)
    slots = src_list.shape[0]
    capacity = max(2, 2 * slots // groups)
    ranks = slot_ranks(src_list)
    all_src, all_ids = (
        lax.all_gather(sources, "dp", axis=0, tiled=True),
        lax.all_gather(block_ids, "dp", axis=0, tiled=True),
    )
    all_src = all_src.reshape(groups, slots)
    owners = jnp.reshape(lax.axis_index("dp"), (1,))
    send_table = owner_table(all_src, all_ids, slot_ranks(all_src), owners, capacity).reshape(
        groups, capacity
    )
    picked = hist_kv[send_table.reshape(-1)]
    block_len = picked.shape[1]
    width = picked.shape[3]
    picked = picked.reshape(groups, capacity, block_len, 2, width)
    where_from = src_list * capacity + ranks
    arrived = lax.all_to_all(picked, "dp", split_axis=0, concat_axis=0, tiled=True)
    arrived = arrived.reshape(groups * capacity, block_len, 2, width)[where_from]
    hist_keys = arrived[:, :, 0]
    hist_vals = arrived[:, :, 1]
    score_scale = 1.0 / math.sqrt(HD)
    step = math.gcd(slots, 8)
    turns = slots // step
    key_blocks = hist_keys.reshape(turns, step * block_len, kv_heads, HD)
    val_blocks = hist_vals.reshape(turns, step * block_len, kv_heads, HD)
    live = jnp.repeat((jnp.arange(slots) < hist_len[0]).reshape(turns, step), block_len, axis=1)
    causal = jnp.arange(new_count)[:, None] >= jnp.arange(new_count)[None, :]
    fresh_turn_scores = (
        jnp.einsum("fusi,pui->usfp", query_rows, key_local_part, preferred_element_type=jnp.float32)
        * score_scale
    )
    fresh_turn_scores = jnp.where(causal[None, None], fresh_turn_scores, -jnp.inf)

    def score_block(keys, mask):
        scores = (
            jnp.einsum("nhgd,khd->hgnk", query_rows, keys, preferred_element_type=jnp.float32)
            * score_scale
        )
        return jnp.where(mask[None, None, None, :], scores, -jnp.inf)

    def max_step(top, inputs):
        keys, mask = inputs
        return (jnp.maximum(top, jnp.max(score_block(keys, mask), axis=-1)), None)

    top, _ = lax.scan(max_step, jnp.max(fresh_turn_scores, axis=-1), (key_blocks, live))

    def sum_step(carry, inputs):
        total, running_sum = carry
        keys, vals, mask = inputs
        weights = jnp.exp(score_block(keys, mask) - top[..., None])
        total = total + jnp.sum(weights, axis=-1)
        running_sum = running_sum + jnp.einsum(
            "hgnk,khd->nhgd", weights.astype(jnp.bfloat16), vals, preferred_element_type=jnp.float32
        )
        return ((total, running_sum), None)

    new_weights = jnp.exp(fresh_turn_scores - top[..., None])
    start_total = jnp.sum(new_weights, axis=-1)
    start_summed = jnp.einsum(
        "vxyl,lvq->yvxq",
        new_weights.astype(jnp.bfloat16),
        v_here,
        preferred_element_type=jnp.float32,
    )
    (total, running_sum), _ = lax.scan(
        sum_step, (start_total, start_summed), (key_blocks, val_blocks, live)
    )
    result = running_sum / jnp.transpose(total, (2, 0, 1))[..., None]
    result = result.astype(jnp.bfloat16).reshape(new_count, 1, kv_heads * per_kv * HD)
    back = lax.all_to_all(result, "tensor", split_axis=0, concat_axis=1, tiled=True)
    return back.reshape(tok_local, q_width)


def solution(mesh):
    return jax.shard_map(
        local,
        mesh=mesh,
        in_specs=(
            P(("dp", "tensor"), None),
            P(("dp", "tensor"), None),
            P(("dp", "tensor"), None),
            P("dp", None, None, "tensor"),
            P("dp", None, None),
            P("dp", None),
            P("dp"),
        ),
        out_specs=P(("dp", "tensor"), None),
        check_vma=False,
    )
```

profile of v0, /device:TPU:1, one launch (start us, length us, event | category | flops | bytes accessed | tf_op | source)
XLA Modules:
  0.0 414.2 jit_solution(10428861804598068745)
XLA Ops:
  1.5 7.7 %all-to-all-start = ((bf16[16,8,128]{2,0,1:T(8,128)(2,1)}), bf16[16,8,128]{2,0,1:T(8,128)(2,1)S(1)}, u32[]{:S(2)}, u32[]{:S(2)}) async-start(bf16[16,8,128]{2,0,1:T(8,128)(2,1)} %copy_bitcast_fusion.2), calls=%async_computation | async-start | bytes 65536 | tf_op jit(solution)/shard_map/all_to_all | solution.py:38
  9.2 45.8 %all_gather.6 = s32[64,64,1]{1,2,0:T(1,128)S(1)} all-gather(s32[1,64,1]{1,2,0:T(1,128)} %param.15), channel_id=1, replica_groups=mesh['dp'=64,'tensor'=8] {'dp'}, dimensions={0}, use_global_device_ids=true | all-gather | bytes 16640 | tf_op jit(solution)/shard_map/all_gather | solution.py:50
  56.6 6.9 %all-to-all-start.1 = ((bf16[16,8,1024]{2,0,1:T(8,128)(2,1)}), bf16[16,8,1024]{2,0,1:T(8,128)(2,1)S(1)}, u32[]{:S(2)}, u32[]{:S(2)}) async-start(bf16[16,8,1024]{2,0,1:T(8,128)(2,1)} %bitcast.179), calls=%async_computation.1 | async-start | bytes 524288 | tf_op jit(solution)/shard_map/all_to_all | solution.py:37
  63.6 1.9 convert_reduce_fusion
  65.4 38.3 %all-gather = s32[64,1,64]{2,1,0:T(1,128)S(1)} all-gather(s32[1,1,64]{2,1,0:T(1,128)} %bitcast.232), channel_id=1, replica_groups=mesh['dp'=64,'tensor'=8] {'dp'}, dimensions={0}, use_global_device_ids=true | all-gather | bytes 16640 | tf_op jit(solution)/shard_map/all_gather | solution.py:51
  104.2 19.5 %gather_fusion = bf16[128,128,2,128]{3,2,1,0:T(2,128)(2,1)} fusion(bf16[32,128,2,128]{3,2,1,0:T(2,128)(2,1)S(1)} %copy-done, s32[1024]{0:T(1024)S(1)} %pad_clamp_fusion.1), kind=kCustom, calls=%fused_computation | custom fusion | bytes 16777728 | tf_op jit(solution)/shard_map/gather | solution.py:58
  123.6 9.1 %copy.77 = bf16[64,2,128,2,128]{4,2,3,1,0:T(8,128)(2,1)} copy(bf16[64,2,128,2,128]{4,3,2,1,0:T(2,128)(2,1)} %bitcast.211) | data formatting | bytes 16777216 | tf_op jit(solution)/shard_map/reshape | solution.py:61
  132.8 7.2 %all-to-all-start.2 = ((bf16[64,2,128,2,128]{4,2,3,1,0:T(8,128)(2,1)}), bf16[64,2,128,2,128]{4,2,3,1,0:T(8,128)(2,1)}, u32[]{:S(2)}, u32[]{:S(2)}) async-start(bf16[64,2,128,2,128]{4,2,3,1,0:T(8,128)(2,1)} %copy.77), calls=%async_computation.2 | async-start | bytes 16777216 | tf_op jit(solution)/shard_map/all_to_all | solution.py:63
  141.9 183.8 %all-to-all-done.2 = bf16[64,2,128,2,128]{4,2,3,1,0:T(8,128)(2,1)} async-done(((bf16[64,2,128,2,128]{4,2,3,1,0:T(8,128)(2,1)}), bf16[64,2,128,2,128]{4,2,3,1,0:T(8,128)(2,1)}, u32[]{:S(2)}, u32[]{:S(2)}) %all-to-all-start.2) | async-done | bytes 8388640 | tf_op jit(solution)/shard_map/all_to_all | solution.py:63
  325.7 6.9 %all-to-all-start.3 = ((bf16[16,8,128]{2,0,1:T(8,128)(2,1)}), bf16[16,8,128]{2,0,1:T(8,128)(2,1)S(1)}, u32[]{:S(2)}, u32[]{:S(2)}) async-start(bf16[16,8,128]{2,0,1:T(8,128)(2,1)} %copy_bitcast_fusion.1), calls=%async_computation.3 | async-start | bytes 65536 | tf_op jit(solution)/shard_map/all_to_all | solution.py:39
  332.6 6.4 %gather_fusion.1 = bf16[64,128,2,128]{3,1,2,0:T(8,128)(2,1)} fusion(bf16[128,128,2,128]{3,1,2,0:T(8,128)(2,1)} %bitcast.34, s32[1024]{0:T(1024)S(1)} %pad_clamp_fusion), kind=kCustom, calls=%fused_computation.1 | custom fusion | bytes 8388864 | tf_op jit(solution)/shard_map/gather | solution.py:64
  339.1 4.7 %fusion.39 = (bf16[64,128,1,128]{3,1,2,0:T(8,128)(2,1)}, bf16[64,128,1,128]{3,1,2,0:T(8,128)(2,1)}) fusion(bf16[64,128,2,128]{3,1,2,0:T(8,128)(2,1)} %gather_fusion.1), kind=kLoop, calls=%fused_computation.63 | loop fusion | bytes 8388608 | tf_op jit(solution)/shard_map/slice | solution.py:66
  343.8 13.9 %while.22 = (s32[]{:T(128)}, f32[1,8,128]{2,1,0:T(8,128)S(1)}, pred[8,1024]{1,0:T(8,128)(4,1)S(1)}, bf16[8,1024,1,128]{3,1,2,0:T(8,128)(2,1)}, bf16[128,1,8,128]{3,0,2,1:T(8,128)(2,1)S(1)}, /*index=5*/s32[]{:T(128)}) while((s32[]{:T(128)}, f32[1,8,128]{2,1,0:T(8,128)S(1)}, pred[8,1024]{1,0:T(8,128)(4,1)S(1)}, ...), condition=%wide.region_6.7_spmd, body=%wide.region_4.6_spmd.sunk | while | flops 271581184 | bytes 544329 | solution.py:91
  347.3 1.7 fusion.54
  358.3 34.3 %while.23 = (s32[]{:T(128)}, f32[1,8,128]{2,1,0:T(8,128)S(1)}, f32[128,1,8,128]{0,3,2,1:T(8,128)S(1)}, pred[8,1024]{1,0:T(8,128)(4,1)S(1)}, bf16[8,1024,1,128]{3...) while((s32[]{:T(128)}, f32[1,8,128]{2,1,0:T(8,128)S(1)}, ...), condition=%wide.region_10.11_spmd, body=%wide.region_8.10_spmd.sunk | while | flops 545390592 | bytes 10253409 | solution.py:111
  358.4 2.0 fusion.57
  360.4 2.2 fusion.58
  362.7 2.1 fusion.57
  364.7 2.2 fusion.58
  367.0 2.1 fusion.57
  369.0 2.2 fusion.58
  371.3 2.1 fusion.57
  373.3 2.2 fusion.58
  375.6 2.1 fusion.57
  377.6 2.2 fusion.58
  379.8 2.1 fusion.57
  381.9 2.2 fusion.58
  384.1 2.1 fusion.57
  386.2 2.2 fusion.58
  388.4 2.1 fusion.57
  390.5 2.2 fusion.58
  394.4 18.7 %all_to_all.65 = bf16[8,2,8192]{2,1,0:T(2,128)(2,1)S(1)} all-to-all(bf16[8,2,8192]{2,1,0:T(2,128)(2,1)S(1)} %reshape.256), channel_id=1, replica_groups=mesh['dp'=64,'tensor'=8] {'tensor'}, dimensions={0} | all-to-all | bytes 524288 | tf_op jit(solution)/shard_map/all_to_all | solution.py:116
  (78 shorter events, 20.4 us)
Async XLA Ops:
  0.0 104.1 %copy-start = (bf16[32,128,2,128]{3,2,1,0:T(2,128)(2,1)S(1)}, bf16[32,128,2,128]{3,2,1,0:T(2,128)(2,1)}, u32[]{:S(2)}) copy-start(bf16[32,128,2,128]{3,2,1,0:T(2,128)(2,1)} %param.14) | copy-start | bytes 6291460
  1.5 55.1 %all-to-all-start = ((bf16[16,8,128]{2,0,1:T(8,128)(2,1)}), bf16[16,8,128]{2,0,1:T(8,128)(2,1)S(1)}, u32[]{:S(2)}, u32[]{:S(2)}) async-start(bf16[16,8,128]{2,0,1:T(8,128)(2,1)} %copy_bitcast_fusion.2), calls=%async_computation | async-start | bytes 65536 | tf_op jit(solution)/shard_map/all_to_all | solution.py:38
  56.6 76.1 %all-to-all-start.1 = ((bf16[16,8,1024]{2,0,1:T(8,128)(2,1)}), bf16[16,8,1024]{2,0,1:T(8,128)(2,1)S(1)}, u32[]{:S(2)}, u32[]{:S(2)}) async-start(bf16[16,8,1024]{2,0,1:T(8,128)(2,1)} %bitcast.179), calls=%async_computation.1 | async-start | bytes 524288 | tf_op jit(solution)/shard_map/all_to_all | solution.py:37
  132.8 7.8 %copy-start.2 = (s32[1,64,1]{1,2,0:T(1,128)S(1)}, s32[1,64,1]{1,2,0:T(1,128)}, u32[]{:S(2)}) copy-start(s32[1,64,1]{1,2,0:T(1,128)} %param.15) | copy-start | bytes 772
  132.8 8.1 %copy-start.1 = (bf16[16,1024]{1,0:T(8,128)(2,1)S(1)}, bf16[16,1024]{1,0:T(8,128)(2,1)}, u32[]{:S(2)}) copy-start(bf16[16,1024]{1,0:T(8,128)(2,1)} %param.13) | copy-start | bytes 98308
  132.8 192.9 %all-to-all-start.2 = ((bf16[64,2,128,2,128]{4,2,3,1,0:T(8,128)(2,1)}), bf16[64,2,128,2,128]{4,2,3,1,0:T(8,128)(2,1)}, u32[]{:S(2)}, u32[]{:S(2)}) async-start(bf16[64,2,128,2,128]{4,2,3,1,0:T(8,128)(2,1)} %copy.77), calls=%async_computation.2 | async-start | bytes 16777216 | tf_op jit(solution)/shard_map/all_to_all | solution.py:63
  325.7 32.1 %all-to-all-start.3 = ((bf16[16,8,128]{2,0,1:T(8,128)(2,1)}), bf16[16,8,128]{2,0,1:T(8,128)(2,1)S(1)}, u32[]{:S(2)}, u32[]{:S(2)}) async-start(bf16[16,8,128]{2,0,1:T(8,128)(2,1)} %copy_bitcast_fusion.1), calls=%async_computation.3 | async-start | bytes 65536 | tf_op jit(solution)/shard_map/all_to_all | solution.py:39
where the time goes:
time: 416 us; the launch traced here: 414 us
  waiting for transfers between devices  184 us (44%)
  blocking collectives  103 us (25%)
  matrix products  47.7 us (11%)
  local copies, waits for them, and re-layouts  46.6 us (11%)
  starting transfers between devices  28.7 us (7%)
    all_to_all x1, waiting for transfers between devices, local(): lax.all_to_all(picked, 'dp', split_axis=0, concat_axis=0, tiled=True)  184 us
    all_gather x1, blocking collectives, local(): lax.all_gather(sources, 'dp', axis=0, tiled=True)  45.8 us
    all_gather x1, blocking collectives, local(): lax.all_gather(block_ids, 'dp', axis=0, tiled=True)  38.3 us
    dot_general x16, matrix products, score_block(): jnp.einsum('nhgd,khd->hgnk', query_rows, keys, preferred_element_type=jnp...  29.8 us
    gather x1, local copies, waits for them, and re-layouts, local(): picked = hist_kv[send_table.reshape(-1)]  19.5 us
    all_to_all x1, blocking collectives, local(): lax.all_to_all(result, 'tensor', split_axis=0, concat_axis=1, tiled=True)  18.7 us
    dot_general x8, matrix products, sum_step(): jnp.einsum('hgnk,khd->nhgd', weights.astype(jnp.bfloat16), vals, preferre...  17.4 us
    reshape x1, local copies, waits for them, and re-layouts, local(): picked = picked.reshape(groups, capacity, block_len, 2, width)  9.15 us
  transfers between devices with their start and end apart: 4, of which 1 were waited for; matrix products, arithmetic and copies ran while one was open for 14% of the time, Pallas kernels for 0%

commit v1 on v0

--- a/solution.py
+++ b/solution.py
@@ -48,7 +48,9 @@
     ranks = slot_ranks(src_list)
     all_src, all_ids = (
         lax.all_gather(sources, "dp", axis=0, tiled=True),
-        lax.all_gather(block_ids, "dp", axis=0, tiled=True),
+        jnp.concatenate(
+            lax.all_to_all(jnp.stack([block_ids] * lax.axis_size("dp")), "dp", 0, 0), axis=0
+        ),
     )
     all_src = all_src.reshape(groups, slots)
     owners = jnp.reshape(lax.axis_index("dp"), (1,))

time: 416 us -> 393 us (0.945)
  blocking collectives: 103 us -> 60.2 us
  starting transfers between devices: 28.7 us -> 40.4 us
  waiting for transfers between devices: 184 us -> 191 us
    all_gather x1 -> x0, blocking collectives: 38.3 us -> none  [local(): lax.all_gather(block_ids, 'dp', axis=0, tiled=True)]
    all_to_all x0 -> x1, starting transfers between devices: none -> 14.8 us  [local(): lax.all_to_all(jnp.stack([block_ids] * lax.axis_size('dp')), 'dp', 0, 0)]
    all_to_all x1, waiting for transfers between devices: 0.01 us -> 6.86 us  [local(): lax.all_to_all(k_parts, 'tensor', split_axis=1, concat_axis=0, tiled=True)]
    all_gather x1, blocking collectives: 45.8 us -> 41.4 us  [local(): lax.all_gather(sources, 'dp', axis=0, tiled=True)]
  transfers between devices with their start and end apart: 4 -> 5, of which waited for: 1 -> 2; matrix products, arithmetic and copies ran while one was open for 14% -> 15% of each run, Pallas kernels for 0% -> 0%
where the time goes in v1:
time: 393 us; the launch traced here: 392 us
  waiting for transfers between devices  191 us (49%)
  blocking collectives  60.2 us (15%)
  local copies, waits for them, and re-layouts  47.8 us (12%)
  matrix products  47.7 us (12%)
  starting transfers between devices  40.4 us (10%)
    all_to_all x1, waiting for transfers between devices, local(): lax.all_to_all(picked, 'dp', split_axis=0, concat_axis=0, tiled=True)  184 us
    all_gather x1, blocking collectives, local(): lax.all_gather(sources, 'dp', axis=0, tiled=True)  41.4 us
    dot_general x16, matrix products, score_block(): jnp.einsum('nhgd,khd->hgnk', query_rows, keys, preferred_element_type=jnp...  29.9 us
    gather x1, local copies, waits for them, and re-layouts, local(): picked = hist_kv[send_table.reshape(-1)]  19.5 us
    all_to_all x1, blocking collectives, local(): lax.all_to_all(result, 'tensor', split_axis=0, concat_axis=1, tiled=True)  18.8 us
    dot_general x8, matrix products, sum_step(): jnp.einsum('hgnk,khd->nhgd', weights.astype(jnp.bfloat16), vals, preferre...  17.4 us
    all_to_all x1, starting transfers between devices, local(): lax.all_to_all(jnp.stack([block_ids] * lax.axis_size('dp')), 'dp', 0, 0)  14.8 us
    reshape x1, local copies, waits for them, and re-layouts, local(): picked = picked.reshape(groups, capacity, block_len, 2, width)  9.15 us
  transfers between devices with their start and end apart: 5, of which 2 were waited for; matrix products, arithmetic and copies ran while one was open for 15% of the time, Pallas kernels for 0%

profile of v1, /device:TPU:1, one launch (start us, length us, event | category | flops | bytes accessed | tf_op | source)
XLA Modules:
  0.0 391.5 jit_solution(3708033605290939067)
XLA Ops:
  1.4 14.8 %all-to-all-start.2 = ((s32[64,1,64]{2,1,0:T(1,128)}), s32[64,1,64]{2,1,0:T(1,128)S(1)}, u32[]{:S(2)}, u32[]{:S(2)}) async-start(s32[64,1,64]{2,1,0:T(1,128)} %stack.2), calls=%async_computation.2 | async-start | bytes 65536 | tf_op jit(solution)/shard_map/all_to_all | solution.py:52
  16.3 41.4 %all_gather.3 = s32[64,64,1]{1,2,0:T(1,128)S(1)} all-gather(s32[1,64,1]{1,2,0:T(1,128)} %param.15), channel_id=1, replica_groups=mesh['dp'=64,'tensor'=8] {'dp'}, dimensions={0}, use_global_device_ids=true | all-gather | bytes 16640 | tf_op jit(solution)/shard_map/all_gather | solution.py:50
  60.7 6.8 %all-to-all-start = ((bf16[16,8,128]{2,0,1:T(8,128)(2,1)}), bf16[16,8,128]{2,0,1:T(8,128)(2,1)S(1)}, u32[]{:S(2)}, u32[]{:S(2)}) async-start(bf16[16,8,128]{2,0,1:T(8,128)(2,1)} %copy_bitcast_fusion.2), calls=%async_computation | async-start | bytes 65536 | tf_op jit(solution)/shard_map/all_to_all | solution.py:38
  67.6 6.9 %all-to-all-done = bf16[16,8,128]{2,0,1:T(8,128)(2,1)S(1)} async-done(((bf16[16,8,128]{2,0,1:T(8,128)(2,1)}), bf16[16,8,128]{2,0,1:T(8,128)(2,1)S(1)}, u32[]{:S(2)}, u32[]{:S(2)}) %all-to-all-start) | async-done | bytes 32800 | tf_op jit(solution)/shard_map/all_to_all | solution.py:38
  74.4 3.4 all-to-all-start.1
  77.9 1.9 convert_reduce_fusion
  80.1 19.5 %gather_fusion = bf16[128,128,2,128]{3,2,1,0:T(2,128)(2,1)} fusion(bf16[32,128,2,128]{3,2,1,0:T(2,128)(2,1)S(1)} %copy-done, s32[1024]{0:T(1024)S(1)} %pad_clamp_fusion.1), kind=kCustom, calls=%fused_computation | custom fusion | bytes 16777728 | tf_op jit(solution)/shard_map/gather | solution.py:60
  99.6 9.1 %copy.77 = bf16[64,2,128,2,128]{4,2,3,1,0:T(8,128)(2,1)} copy(bf16[64,2,128,2,128]{4,3,2,1,0:T(2,128)(2,1)} %bitcast.211) | data formatting | bytes 16777216 | tf_op jit(solution)/shard_map/reshape | solution.py:63
  108.7 8.5 %all-to-all-start.3 = ((bf16[64,2,128,2,128]{4,2,3,1,0:T(8,128)(2,1)}), bf16[64,2,128,2,128]{4,2,3,1,0:T(8,128)(2,1)}, u32[]{:S(2)}, u32[]{:S(2)}) async-start(bf16[64,2,128,2,128]{4,2,3,1,0:T(8,128)(2,1)} %copy.77), calls=%async_computation.3 | async-start | bytes 16777216 | tf_op jit(solution)/shard_map/all_to_all | solution.py:65
  119.2 183.8 %all-to-all-done.3 = bf16[64,2,128,2,128]{4,2,3,1,0:T(8,128)(2,1)} async-done(((bf16[64,2,128,2,128]{4,2,3,1,0:T(8,128)(2,1)}), bf16[64,2,128,2,128]{4,2,3,1,0:T(8,128)(2,1)}, u32[]{:S(2)}, u32[]{:S(2)}) %all-to-all-start.3) | async-done | bytes 8388640 | tf_op jit(solution)/shard_map/all_to_all | solution.py:65
  303.0 6.8 %all-to-all-start.4 = ((bf16[16,8,128]{2,0,1:T(8,128)(2,1)}), bf16[16,8,128]{2,0,1:T(8,128)(2,1)S(1)}, u32[]{:S(2)}, u32[]{:S(2)}) async-start(bf16[16,8,128]{2,0,1:T(8,128)(2,1)} %copy_bitcast_fusion.1), calls=%async_computation.4 | async-start | bytes 65536 | tf_op jit(solution)/shard_map/all_to_all | solution.py:39
  309.9 6.4 %gather_fusion.1 = bf16[64,128,2,128]{3,1,2,0:T(8,128)(2,1)} fusion(bf16[128,128,2,128]{3,1,2,0:T(8,128)(2,1)} %bitcast.34, s32[1024]{0:T(1024)S(1)} %pad_clamp_fusion), kind=kCustom, calls=%fused_computation.1 | custom fusion | bytes 8388864 | tf_op jit(solution)/shard_map/gather | solution.py:66
  316.3 4.7 %fusion.39 = (bf16[64,128,1,128]{3,1,2,0:T(8,128)(2,1)}, bf16[64,128,1,128]{3,1,2,0:T(8,128)(2,1)}) fusion(bf16[64,128,2,128]{3,1,2,0:T(8,128)(2,1)} %gather_fusion.1), kind=kLoop, calls=%fused_computation.63 | loop fusion | bytes 8388608 | tf_op jit(solution)/shard_map/slice | solution.py:68
  321.0 13.9 %while.22 = (s32[]{:T(128)}, f32[1,8,128]{2,1,0:T(8,128)S(1)}, pred[8,1024]{1,0:T(8,128)(4,1)S(1)}, bf16[8,1024,1,128]{3,1,2,0:T(8,128)(2,1)}, bf16[128,1,8,128]{3,0,2,1:T(8,128)(2,1)S(1)}, /*index=5*/s32[]{:T(128)}) while((s32[]{:T(128)}, f32[1,8,128]{2,1,0:T(8,128)S(1)}, pred[8,1024]{1,0:T(8,128)(4,1)S(1)}, ...), condition=%wide.region_6.7_spmd, body=%wide.region_4.6_spmd.sunk | while | flops 271581184 | bytes 544329 | solution.py:93
  335.6 34.4 %while.23 = (s32[]{:T(128)}, f32[1,8,128]{2,1,0:T(8,128)S(1)}, f32[128,1,8,128]{0,3,2,1:T(8,128)S(1)}, pred[8,1024]{1,0:T(8,128)(4,1)S(1)}, bf16[8,1024,1,128]{3...) while((s32[]{:T(128)}, f32[1,8,128]{2,1,0:T(8,128)S(1)}, ...), condition=%wide.region_10.11_spmd, body=%wide.region_8.10_spmd.sunk | while | flops 545390592 | bytes 10253409 | solution.py:113
  335.6 2.1 fusion.57
  337.7 2.2 fusion.58
  339.9 2.1 fusion.57
  342.0 2.2 fusion.58
  344.2 2.1 fusion.57
  346.3 2.2 fusion.58
  348.5 2.1 fusion.57
  350.5 2.2 fusion.58
  352.8 2.1 fusion.57
  354.8 2.2 fusion.58
  357.1 2.1 fusion.57
  359.1 2.2 fusion.58
  361.4 2.1 fusion.57
  363.4 2.2 fusion.58
  365.7 2.1 fusion.57
  367.7 2.2 fusion.58
  371.7 18.8 %all_to_all.70 = bf16[8,2,8192]{2,1,0:T(2,128)(2,1)S(1)} all-to-all(bf16[8,2,8192]{2,1,0:T(2,128)(2,1)S(1)} %reshape.257), channel_id=1, replica_groups=mesh['dp'=64,'tensor'=8] {'tensor'}, dimensions={0} | all-to-all | bytes 524288 | tf_op jit(solution)/shard_map/all_to_all | solution.py:118
  (80 shorter events, 23.4 us)
Async XLA Ops:
  0.0 80.1 %copy-start = (bf16[32,128,2,128]{3,2,1,0:T(2,128)(2,1)S(1)}, bf16[32,128,2,128]{3,2,1,0:T(2,128)(2,1)}, u32[]{:S(2)}) copy-start(bf16[32,128,2,128]{3,2,1,0:T(2,128)(2,1)} %param.14) | copy-start | bytes 6291460
  1.4 59.3 %all-to-all-start.2 = ((s32[64,1,64]{2,1,0:T(1,128)}), s32[64,1,64]{2,1,0:T(1,128)S(1)}, u32[]{:S(2)}, u32[]{:S(2)}) async-start(s32[64,1,64]{2,1,0:T(1,128)} %stack.2), calls=%async_computation.2 | async-start | bytes 65536 | tf_op jit(solution)/shard_map/all_to_all | solution.py:52
  60.7 13.7 %all-to-all-start = ((bf16[16,8,128]{2,0,1:T(8,128)(2,1)}), bf16[16,8,128]{2,0,1:T(8,128)(2,1)S(1)}, u32[]{:S(2)}, u32[]{:S(2)}) async-start(bf16[16,8,128]{2,0,1:T(8,128)(2,1)} %copy_bitcast_fusion.2), calls=%async_computation | async-start | bytes 65536 | tf_op jit(solution)/shard_map/all_to_all | solution.py:38
  74.4 34.3 %all-to-all-start.1 = ((bf16[16,8,1024]{2,0,1:T(8,128)(2,1)}), bf16[16,8,1024]{2,0,1:T(8,128)(2,1)S(1)}, u32[]{:S(2)}, u32[]{:S(2)}) async-start(bf16[16,8,1024]{2,0,1:T(8,128)(2,1)} %bitcast.179), calls=%async_computation.1 | async-start | bytes 524288 | tf_op jit(solution)/shard_map/all_to_all | solution.py:37
  108.7 9.2 %copy-start.2 = (s32[1,64,1]{1,2,0:T(1,128)S(1)}, s32[1,64,1]{1,2,0:T(1,128)}, u32[]{:S(2)}) copy-start(s32[1,64,1]{1,2,0:T(1,128)} %param.15) | copy-start | bytes 772
  108.7 9.5 %copy-start.1 = (bf16[16,1024]{1,0:T(8,128)(2,1)S(1)}, bf16[16,1024]{1,0:T(8,128)(2,1)}, u32[]{:S(2)}) copy-start(bf16[16,1024]{1,0:T(8,128)(2,1)} %param.13) | copy-start | bytes 98308
  108.7 194.3 %all-to-all-start.3 = ((bf16[64,2,128,2,128]{4,2,3,1,0:T(8,128)(2,1)}), bf16[64,2,128,2,128]{4,2,3,1,0:T(8,128)(2,1)}, u32[]{:S(2)}, u32[]{:S(2)}) async-start(bf16[64,2,128,2,128]{4,2,3,1,0:T(8,128)(2,1)} %copy.77), calls=%async_computation.3 | async-start | bytes 16777216 | tf_op jit(solution)/shard_map/all_to_all | solution.py:65
  303.0 32.1 %all-to-all-start.4 = ((bf16[16,8,128]{2,0,1:T(8,128)(2,1)}), bf16[16,8,128]{2,0,1:T(8,128)(2,1)S(1)}, u32[]{:S(2)}, u32[]{:S(2)}) async-start(bf16[16,8,128]{2,0,1:T(8,128)(2,1)} %copy_bitcast_fusion.1), calls=%async_computation.4 | async-start | bytes 65536 | tf_op jit(solution)/shard_map/all_to_all | solution.py:39
